TPU v7x, 512 devices: a whole 4x4x16 slice. The times are simulated.
512 devices in a mesh: loop: 8 (over y_hi, x), inner: 64 (over z, y_lo, core).
Axes of the slice: x: 4, y: 4 (y_hi: 2, y_lo: 2; y = y_hi * 2 + y_lo), z: 16, core: 2. Of those that a mesh axis runs over, the one named last changes fastest.
Arguments:
- site_blocks: bfloat16 [8, 64, 4, 256, 256], P('loop', 'inner'), may hold values from -6 to 6
- bond_weights: float32 [8, 64, 256], P('loop', 'inner'), may hold values from 0.2 to 2
- bond_gates: float32 [8, 16, 16], P('loop'), may hold values from -3 to 3
- kept_slots: int32 [8, 64], P('loop', 'inner'), may hold values from 64 to 256, as said below
Outputs:
- new_sites: bfloat16 [8, 64, 4, 256, 256], P('loop', 'inner')
- new_weights: float32 [8, 64, 256], P('loop', 'inner')
Inputs may be any that keep to these rules, and one draw needn't show every extreme that they name: `kept_slots`: every bond has at least one sector block with all 256 slots kept.
All inputs are finite; a program needn't handle non-finite values.
Results may differ from a plain program's by a relative error of at most 0.015.
The roundings to bfloat16 on the way count: a program that leaves them out, or rounds other values in their place, can miss the bound.
Values may be sent and summed in bfloat16 or wider, within the bound.
A program may use at most 64 MiB of HBM per device.

v0:
```python
import functools

import jax
import jax.numpy as jnp
from jax import lax
from jax.experimental import pallas as pl
from jax.experimental.pallas import tpu as pltpu
from jax.sharding import PartitionSpec as P

HI = lax.Precision.HIGHEST
NN = (((1,), (0,)), ((), ()))
NT = (((1,), (1,)), ((), ()))
MESH = pl.DeviceIdType.MESH
SLOTS = 256
CHARGE = (0, 1, 1, 2)

LEFT_AT = {-1: {0: 0, 1: 1, 2: 2}, 0: {0: 3, 1: 4, 2: 5, 3: 6}, 1: {1: 7, 2: 8, 3: 9}}
RIGHT_AT = {-1: {1: 1, 2: 2, 3: 6}, 0: {0: 0, 1: 4, 2: 5, 3: 9}, 1: {0: 3, 1: 7, 2: 8}}
PAIRS = [(d, a, b) for d in (-1, 0, 1) for a in LEFT_AT[d] for b in RIGHT_AT[d]]
THETA_AT = {key: n for n, key in enumerate(PAIRS)}


def even(number):
    return 1 - number % 2


def sends(phase, loop, inner):
    home = lambda bond, sector: (bond + even(sector), sector)
    bond = loop - even(inner)
    found = []
    if phase == 0:
        for slot, step in enumerate((1, 0, -1)):
            found.append(("meta_in", 0, 8, "meta", 8 * slot, home(loop, inner + step)))
        if loop % 2 == 0:
            for step, at, size, to in ((1, 0, 3, 0), (0, 0, 4, 3), (-1, 1, 3, 7)):
                found.append(("site", at, size, "left", to, home(loop, inner + step)))
        else:
            for step, at, size, to in ((0, 0, 3, 0), (-1, 0, 4, 3), (-2, 1, 3, 7)):
                found.append(("site", at, size, "right", to, home(loop - 1, inner + step)))
    elif phase == 1 and bond % 2 == 0:
        for step, at, size, to in ((0, 0, 1, 3), (0, 1, 2, 7), (1, 0, 1, 0), (1, 1, 2, 4), (1, 3, 1, 9), (2, 1, 2, 1), (2, 3, 1, 6)):
            found.append(("new_right", at, size, "left", to, home(bond + 1, inner + step)))
        for step, at, size, to in ((0, 0, 3, 0), (-1, 0, 4, 3), (-2, 1, 3, 7)):
            found.append(("new_left", at, size, "right", to, home(bond - 1, inner + step)))
        for step in (0, 1, 2):
            found.append(("level", 0, 8, "levels", 8 * step, home(bond + 1, inner + step)))
        found.append(("level", 0, 8, "weights", 0, (bond, inner)))
    elif phase == 2 and bond % 2 == 1:
        found.append(("new_left", 0, 4, "sites", 0, (bond, inner)))
        for step, at, size in ((0, 0, 1), (1, 1, 2), (2, 3, 1)):
            found.append(("new_right", at, size, "sites", at, (bond + 1, inner + step)))
        found.append(("level", 0, 8, "weights", 0, (bond, inner)))
    if phase == 2 and loop % 2 == 0:
        found.append(("early", 0, 8, "weights", 0, (loop, inner)))
    return [f[:5] + ((f[5][0] - loop, f[5][1] - inner),) for f in found]


def arrivals(phase, loop, inner):
    found = []
    for far in range(-3, 4):
        for away in range(-3, 4):
            for _, _, size, to, at, (x, y) in sends(phase, loop + far, inner + away):
                if (far + x, away + y) == (0, 0):
                    found.append((to, at, size, (far, away)))
    return found


def landings(phase):
    spots = set()
    for kind in range(4):
        spots |= {a[:3] for a in arrivals(phase, 4 + kind // 2, 4 + kind % 2)}
    return sorted(spots)


def partners(phase, loop, inner):
    known = {s[5] for s in sends(phase, loop, inner)} | {a[3] for a in arrivals(phase, loop, inner)}
    return sorted(known - {(0, 0)})


def exchange(phase, refs, barrier, send_sems, recv_sems):
    loop, inner = lax.axis_index("loop"), lax.axis_index("inner")
    rounds, sectors = lax.axis_size("loop"), lax.axis_size("inner")
    spots = landings(phase)

    def device(offset):
        return (lax.rem(loop + offset[0] + rounds, rounds), lax.rem(inner + offset[1] + sectors, sectors))

    for kind in range(4):
        at = (4 + kind // 2, 4 + kind % 2)

        @pl.when((lax.rem(loop, 2) == kind // 2) & (lax.rem(inner, 2) == kind % 2))
        def _(at=at):
            friends = partners(phase, *at)
            for offset in friends:
                pl.semaphore_signal(barrier, inc=1, device_id=device(offset), device_id_type=MESH)
            pl.semaphore_wait(barrier, len(friends))
            copies = []
            for n, (source, first, size, to, where, offset) in enumerate(sends(phase, *at)):
                src, dst = refs[source].at[pl.ds(first, size)], refs[to].at[pl.ds(where, size)]
                slot = recv_sems.at[spots.index((to, where, size))]
                if offset == (0, 0):
                    copy = pltpu.make_async_copy(src, dst, slot)
                else:
                    copy = pltpu.make_async_remote_copy(src, dst, send_sems.at[n], slot, device_id=device(offset), device_id_type=MESH)
                    copies.append(copy)
                copy.start()
            for to, where, size, offset in arrivals(phase, *at):
                dst = refs[to].at[pl.ds(where, size)]
                pltpu.make_async_copy(dst, dst, recv_sems.at[spots.index((to, where, size))]).wait()
            for copy in copies:
                copy.wait_send()


def exchange_call(phase, sources, targets):
    names, shapes = list(sources), list(targets)

    def body(*refs):
        exchange(phase, dict(zip(names + shapes, refs)), pltpu.get_barrier_semaphore(), *refs[-2:])

    most = max(len(sends(phase, 4 + kind // 2, 4 + kind % 2)) for kind in range(4))
    results = pl.pallas_call(
        body,
        out_shape=tuple(targets.values()),
        in_specs=[pl.BlockSpec(memory_space=pl.ANY)] * len(names),
        out_specs=tuple([pl.BlockSpec(memory_space=pl.ANY)] * len(shapes)),
        scratch_shapes=[pltpu.SemaphoreType.DMA((most,)), pltpu.SemaphoreType.DMA((len(landings(phase)),))],
        compiler_params=pltpu.CompilerParams(collective_id=phase, has_side_effects=True),
    )(*sources.values())
    return dict(zip(shapes, results))


def terms_of(outer_a, outer_b):
    found = []
    for d, a, b in PAIRS:
        if CHARGE[a] - CHARGE[outer_a] == d and CHARGE[outer_b] - CHARGE[b] == d:
            found.append(((outer_a * 4 + outer_b) * 16 + a * 4 + b, THETA_AT[d, a, b]))
    return found


def invert_leaf(work):
    n = 128
    lane = lax.broadcasted_iota(jnp.int32, (8, n), 1)
    sub = lax.broadcasted_iota(jnp.int32, (8, n), 0)
    tiles = [work[8 * t:8 * t + 8, :] for t in range(n // 8)]
    for g in range(n // 8):
        k = 8 * g
        cols = {}
        for t in range(g, n // 8):
            cols[t] = [jnp.broadcast_to(tiles[t][:, k + j:k + j + 1], (8, n)) for j in range(8)]
        fresh = (lane >= k) & (lane < k + 8)
        head = jnp.where(fresh, jnp.where(lane - k == sub, 1.0, 0.0), tiles[g])
        for t in range(g + 1, n // 8):
            tiles[t] = jnp.where(fresh, 0.0, tiles[t])
        rows = []
        for j in range(8):
            scale = lax.rsqrt(jnp.broadcast_to(cols[g][j][j:j + 1, :], (8, n)))
            for t in range(g, n // 8):
                cols[t][j] = cols[t][j] * scale
            low = jnp.where(sub > j, cols[g][j], 0.0)
            for i in range(j + 1, 8):
                other = jnp.broadcast_to(low[i:i + 1, :], (8, n))
                for t in range(g, n // 8):
                    cols[t][i] = cols[t][i] - (low if t == g else cols[t][j]) * other
            row = jnp.broadcast_to(head[j:j + 1, :], (8, n)) * scale
            rows.append(row)
            head = jnp.where(sub == j, row, head - low * row)
        for t in range(g + 1, n // 8):
            total = tiles[t]
            for j in range(8):
                total = total - cols[t][j] * rows[j]
            tiles[t] = total
        work[8 * g:8 * g + 8, :] = jnp.where(lane <= sub + k, head, 0.0)


def task(last, meta, left, right, levels, new_left, new_right, level, theta, matrix, proj, gram, work, scaled, numbers, sem):
    n = SLOTS
    copy = pltpu.make_async_copy(meta.at[pl.ds(8, 8)], numbers, sem)
    copy.start()
    for d, at in LEFT_AT.items():
        row = meta[8 * (d + 1):8 * (d + 1) + 1, :]
        for k in at.values():
            scaled[k] = (left[k].astype(jnp.float32) * row).astype(jnp.bfloat16)
    for d, a, b in PAIRS:
        product = jnp.dot(scaled[LEFT_AT[d][a]], right[RIGHT_AT[d][b]], preferred_element_type=jnp.float32)
        theta[THETA_AT[d, a, b]] = (product * (1.0 / 16.0)).astype(jnp.bfloat16)
    copy.wait()

    @pl.loop(0, n // 16)
    def _(step):
        r = pl.multiple_of(step * 16, 16)
        for a in range(4):
            for b in range(4):
                total = None
                for g, t in terms_of(a, b):
                    term = theta[t, pl.ds(r, 16), :].astype(jnp.float32) * numbers[2, g]
                    total = term if total is None else total + term
                matrix[pl.ds(pl.multiple_of(a * n + r, 16), 16), b * n:(b + 1) * n] = total.astype(jnp.bfloat16)

    down = lax.broadcasted_iota(jnp.int32, (n, n), 0)
    diagonal = down == lax.broadcasted_iota(jnp.int32, (n, n), 1)
    total = None
    for a in range(4):
        part = jnp.dot(left[3 + a].T, matrix[a * n:(a + 1) * n, :], preferred_element_type=jnp.float32)
        total = part if total is None else total + part
    row_number = lax.broadcasted_iota(jnp.int32, (n, 4 * n), 0).astype(jnp.float32)
    proj[...] = jnp.where(row_number < numbers[1, 0], total, 0.0)
    dot = functools.partial(lax.dot_general, precision=HI, preferred_element_type=jnp.float32)
    gram[...] = dot(proj[...], proj[...], NT) + jnp.where(diagonal, 1.0, 0.0)
    h = n // 2
    work[...] = gram[:h, :h]
    invert_leaf(work)
    first = work[...]
    lower = dot(gram[h:, :h], first, NT)
    top = dot(first, proj[:h, :], NN)
    work[...] = gram[h:, h:] - dot(lower, lower, NT)
    proj[h:, :] = proj[h:, :] - dot(lower, top, NN)
    proj[:h, :] = top
    invert_leaf(work)
    proj[h:, :] = dot(work[...], proj[h:, :], NN)
    iso = (proj[...] * 32.0).astype(jnp.bfloat16)
    carried = []
    squares = jnp.zeros((1, n), jnp.float32)
    for a in range(4):
        part = lax.dot_general(matrix[a * n:(a + 1) * n, :], iso, NT, preferred_element_type=jnp.float32) * (1.0 / 32.0)
        carried.append(part)
        squares = squares + jnp.sum(part * part, axis=0, keepdims=True)
    lev = jnp.sqrt(squares * (1.0 / 1024.0) + 1e-6)
    level[...] = jnp.broadcast_to(lev, (8, n))

    def upright(row):
        return jnp.sum(jnp.where(diagonal, row, 0.0), axis=1, keepdims=True)

    right_scale = upright(lev) if last else None
    for a in range(4):
        block = (carried[a] / lev).astype(jnp.bfloat16)
        other = iso[:, a * n:(a + 1) * n]
        if last:
            block = (block.astype(jnp.float32) * upright(levels[8 * CHARGE[a]:8 * CHARGE[a] + 1, :])).astype(jnp.bfloat16)
            other = (other.astype(jnp.float32) * right_scale).astype(jnp.bfloat16)
        new_left[a] = block
        new_right[a] = other


def task_call(last, meta, left, right, levels):
    def body(meta, left, right, levels, *others):
        @pl.when(lax.rem(lax.axis_index("loop") + lax.axis_index("inner"), 2) == (0 if last else 1))
        def _():
            task(last, meta, left, right, levels, *others)

    vmem = pl.BlockSpec(memory_space=pltpu.VMEM)
    n = SLOTS
    results = pl.pallas_call(
        body,
        out_shape=(
            jax.ShapeDtypeStruct((4, n, n), jnp.bfloat16),
            jax.ShapeDtypeStruct((4, n, n), jnp.bfloat16),
            jax.ShapeDtypeStruct((8, n), jnp.float32),
        ),
        in_specs=[vmem] * 4,
        out_specs=(vmem,) * 3,
        scratch_shapes=[
            pltpu.VMEM((len(PAIRS), n, n), jnp.bfloat16),
            pltpu.VMEM((4 * n, 4 * n), jnp.bfloat16),
            pltpu.VMEM((n, 4 * n), jnp.float32),
            pltpu.VMEM((n, n), jnp.float32),
            pltpu.VMEM((n // 2, n // 2), jnp.float32),
            pltpu.VMEM((10, n, n), jnp.bfloat16),
            pltpu.SMEM((8, n), jnp.float32),
            pltpu.SemaphoreType.DMA,
        ],
        compiler_params=pltpu.CompilerParams(vmem_limit_bytes=48 << 20),
    )(meta, left, right, levels)
    return dict(zip(("new_left", "new_right", "level"), results))


def per_device(site_blocks, bond_weights, bond_gates, kept_slots):
    n = SLOTS
    gates = lax.reduce_precision(bond_gates.reshape(1, n), 8, 7)
    kept = jnp.broadcast_to(kept_slots.astype(jnp.float32), (1, n))
    meta = jnp.concatenate([bond_weights[0], kept, gates, jnp.zeros((5, n), jnp.float32)], axis=0)
    blocks = lambda count: jax.ShapeDtypeStruct((count, n, n), jnp.bfloat16)
    rows = lambda count: jax.ShapeDtypeStruct((count, n), jnp.float32)
    got = exchange_call(0, {"site": site_blocks[0, 0], "meta_in": meta}, {"left": blocks(10), "right": blocks(10), "meta": rows(24)})
    first = task_call(False, got["meta"], got["left"], got["right"], got["meta"])
    then = exchange_call(1, first, {"left": blocks(10), "right": blocks(10), "levels": rows(24), "weights": rows(8)})
    second = task_call(True, got["meta"], then["left"], then["right"], then["levels"])
    second["early"] = then["weights"]
    final = exchange_call(2, second, {"sites": blocks(4), "weights": rows(8)})
    return (final["sites"][None, None], final["weights"][None, :1])


def solution(mesh):
    return jax.shard_map(
        per_device,
        mesh=mesh,
        in_specs=(
            P("loop", "inner", None, None, None),
            P("loop", "inner", None),
            P("loop", None, None),
            P("loop", "inner"),
        ),
        out_specs=(P("loop", "inner", None, None, None), P("loop", "inner", None)),
        check_vma=False,
    )
```

profile of v0, /device:TPU:7, one launch (start us, length us, event | category | flops | bytes accessed | tf_op | source)
XLA Modules:
  0.0 119.3 jit_solution(5139378852011905099)
XLA Ops:
  1.3 0.1 pad.1.clone
  1.4 0.1 pad.3.clone
  1.4 0.7 reduce_precision.14
  2.1 0.1 reduce_precision.15
  2.2 1.4 %maximum_maximum_fusion.refs_1_ = f32[8,256]{1,0:T(8,128)} fusion(f32[1,256]{1,0:T(1,128)S(1)} %reduce_precision.15, f32[1,256]{1,0:T(1,128)} %bitcast.10, f32[8]{0:T(128)S(1)} %pad.3.clone, f32[8]{0:T(128)S(1)} %pad.1.clone), kind=kLoop, calls=%fused_computation | loop fusion | flops 6144 | bytes 10304 | tf_op jit(solution)/shard_map/concatenate | solution.py:280
  3.6 23.6 %shard_map.59 = (bf16[10,256,256]{2,1,0:T(8,128)(2,1)}, bf16[10,256,256]{2,1,0:T(8,128)(2,1)}, f32[24,256]{1,0:T(8,128)}) custom-call(bf16[4,256,256]{2,1,0:T(8,128)(2,1)} %bitcast.8, f32[8,256]{1,0:T(8,128)} %maximum_maximum_fusion.refs_1_), custom_call_target="tpu_custom_call" | custom-call | tf_op jit(solution)/shard_map/pallas_call | solution.py:121
  27.1 1.3 %copy-done.2 = bf16[10,256,256]{2,1,0:T(8,128)(2,1)S(1)} copy-done((bf16[10,256,256]{2,1,0:T(8,128)(2,1)S(1)}, bf16[10,256,256]{2,1,0:T(8,128)(2,1)}, u32[]{:S(2)}) %copy-start.2) | copy-done | bytes 1310744
  28.4 1.3 %copy-done.3 = bf16[10,256,256]{2,1,0:T(8,128)(2,1)S(1)} copy-done((bf16[10,256,256]{2,1,0:T(8,128)(2,1)S(1)}, bf16[10,256,256]{2,1,0:T(8,128)(2,1)}, u32[]{:S(2)}) %copy-start.3) | copy-done | bytes 1310744
  29.8 0.7 copy-done.8
  30.5 0.0 copy-start.6
  30.5 0.8 copy-done.6
  31.3 0.8 copy-done.7
  32.1 0.6 copy-done.12
  32.7 37.1 %shard_map.61 = (bf16[10,256,256]{2,1,0:T(8,128)(2,1)}, bf16[10,256,256]{2,1,0:T(8,128)(2,1)}, f32[24,256]{1,0:T(8,128)}, f32[8,256]{1,0:T(8,128)}) custom-call(bf16[4,256,256]{2,1,0:T(8,128)(2,1)} %copy-done.6, bf16[4,256,256]{2,1,0:T(8,128)(2,1)} %copy-done.7, f32[8,256]{1,0:T(8,128)} %copy-done.12), custom_call_target="tpu_custom_call" | custom-call | tf_op jit(solution)/shard_map/pallas_call | solution.py:121
  69.9 1.3 %copy-done = bf16[10,256,256]{2,1,0:T(8,128)(2,1)S(1)} copy-done((bf16[10,256,256]{2,1,0:T(8,128)(2,1)S(1)}, bf16[10,256,256]{2,1,0:T(8,128)(2,1)}, u32[]{:S(2)}) %copy-start) | copy-done | bytes 1310744
  71.2 1.3 %copy-done.1 = bf16[10,256,256]{2,1,0:T(8,128)(2,1)S(1)} copy-done((bf16[10,256,256]{2,1,0:T(8,128)(2,1)S(1)}, bf16[10,256,256]{2,1,0:T(8,128)(2,1)}, u32[]{:S(2)}) %copy-start.1) | copy-done | bytes 1310744
  72.5 0.7 copy-done.10
  73.2 16.0 %shard_map.62 = (bf16[4,256,256]{2,1,0:T(8,128)(2,1)S(1)}, bf16[4,256,256]{2,1,0:T(8,128)(2,1)S(1)}, f32[8,256]{1,0:T(8,128)S(1)}) custom-call(f32[24,256]{1,0:T(8,128)S(1)} %copy-done.9, bf16[10,256,256]{2,1,0:T(8,128)(2,1)S(1)} %copy-done, bf16[10,256,256]{2,1,0:T(8,128)(2,1)S(1)} %copy-done.1, f32[24,256]{1,0:T(8,128)S(1)} %copy-done.10), custom_call_target="tpu_custom_call" | custom-call | tf_op jit(solution)/shard_map/pallas_call | solution.py:252
  89.3 0.8 copy-done.4
  90.1 0.8 copy-done.5
  90.9 0.6 copy-done.11
  91.5 24.7 %shard_map.63 = (bf16[4,256,256]{2,1,0:T(8,128)(2,1)}, f32[8,256]{1,0:T(8,128)}) custom-call(bf16[4,256,256]{2,1,0:T(8,128)(2,1)} %copy-done.4, bf16[4,256,256]{2,1,0:T(8,128)(2,1)} %copy-done.5, f32[8,256]{1,0:T(8,128)} %copy-done.11, f32[8,256]{1,0:T(8,128)} %get-tuple-element.29.refs_3_), custom_call_target="tpu_custom_call" | custom-call | tf_op jit(solution)/shard_map/pallas_call | solution.py:121
  116.2 1.3 %slice_bitcast_fusion = f32[1,1,256]{2,1,0:T(1,128)} fusion(f32[8,256]{1,0:T(8,128)} %get-tuple-element.31), kind=kLoop, calls=%fused_computation.1 | loop fusion | bytes 2048 | tf_op jit(solution)/shard_map/broadcast_in_dim | solution.py:289
  117.4 1.9 %copy.8 = bf16[1,1,4,256,256]{4,3,2,1,0:T(8,128)(2,1)} copy(bf16[1,1,4,256,256]{4,3,2,1,0:T(8,128)(2,1)} %bitcast.9) | data formatting | bytes 1048576
  (15 shorter events, 0.0 us)
Async XLA Ops:
  27.1 1.3 %copy-start.2 = (bf16[10,256,256]{2,1,0:T(8,128)(2,1)S(1)}, bf16[10,256,256]{2,1,0:T(8,128)(2,1)}, u32[]{:S(2)}) copy-start(bf16[10,256,256]{2,1,0:T(8,128)(2,1)} %get-tuple-element.18.left) | copy-start | bytes 3932164
  28.4 1.3 %copy-start.3 = (bf16[10,256,256]{2,1,0:T(8,128)(2,1)S(1)}, bf16[10,256,256]{2,1,0:T(8,128)(2,1)}, u32[]{:S(2)}) copy-start(bf16[10,256,256]{2,1,0:T(8,128)(2,1)} %get-tuple-element.19.right) | copy-start | bytes 3932164
  29.8 0.7 copy-start.8
  30.5 39.4 %copy-start.9 = (f32[24,256]{1,0:T(8,128)S(1)}, f32[24,256]{1,0:T(8,128)}, u32[]{:S(2)}) copy-start(f32[24,256]{1,0:T(8,128)} %get-tuple-element.17.meta.levels) | copy-start | bytes 73732
  30.5 0.8 copy-start.6
  31.3 0.8 copy-start.7
  32.1 0.6 copy-start.12
  69.9 1.3 %copy-start = (bf16[10,256,256]{2,1,0:T(8,128)(2,1)S(1)}, bf16[10,256,256]{2,1,0:T(8,128)(2,1)}, u32[]{:S(2)}) copy-start(bf16[10,256,256]{2,1,0:T(8,128)(2,1)} %get-tuple-element.23.left) | copy-start | bytes 3932164
  71.2 1.3 %copy-start.1 = (bf16[10,256,256]{2,1,0:T(8,128)(2,1)S(1)}, bf16[10,256,256]{2,1,0:T(8,128)(2,1)}, u32[]{:S(2)}) copy-start(bf16[10,256,256]{2,1,0:T(8,128)(2,1)} %get-tuple-element.24.right) | copy-start | bytes 3932164
  72.5 0.7 copy-start.10
  89.3 0.8 copy-start.4
  90.1 0.8 copy-start.5
  90.9 0.6 copy-start.11
where the time goes:
time: 120 us; the launch traced here: 119 us
  Pallas kernels  101 us (84%)
  local copies, waits for them, and re-layouts  14.4 us (12%)
  other arithmetic  2.05 us (2%)
  between operations  1.37 us (1%)
    pallas_call x3, Pallas kernels, exchange_call(): pl.pallas_call(body, out_shape=tuple(targets.values()), in_specs=[pl.Bloc...  85.4 us
    pallas_call x2, Pallas kernels, task_call(): pl.pallas_call(body, out_shape=(jax.ShapeDtypeStruct((4, n, n), jnp.bfloa...  16 us
    unnamed x27, local copies, waits for them, and re-layouts  13 us

commit v1 on v0

v1 whole, which is shorter than its diff:
```python
import functools

import jax
import jax.numpy as jnp
from jax import lax
from jax.experimental import pallas as pl
from jax.experimental.pallas import tpu as pltpu
from jax.sharding import PartitionSpec as P

HI = lax.Precision.HIGHEST
NN = (((1,), (0,)), ((), ()))
NT = (((1,), (1,)), ((), ()))
MESH = pl.DeviceIdType.MESH
SLOTS = 256
CHARGE = (0, 1, 1, 2)

LEFT_AT = {-1: {0: 0, 1: 1, 2: 2}, 0: {0: 3, 1: 4, 2: 5, 3: 6}, 1: {1: 7, 2: 8, 3: 9}}
RIGHT_AT = {-1: {1: 1, 2: 2, 3: 6}, 0: {0: 0, 1: 4, 2: 5, 3: 9}, 1: {0: 3, 1: 7, 2: 8}}
PAIRS = [(d, a, b) for d in (-1, 0, 1) for a in LEFT_AT[d] for b in RIGHT_AT[d]]
THETA_AT = {key: n for n, key in enumerate(PAIRS)}


def even(number):
    return 1 - number % 2


def sends(phase, loop, inner):
    home = lambda bond, sector: (bond + even(sector), sector)
    bond = loop - even(inner)
    found = []
    if phase == 0:
        if loop % 2 == 0:
            for step, at, size, to in ((-1, 1, 3, 7), (1, 0, 3, 0), (0, 0, 4, 3)):
                found.append(("site", at, size, "left", to, home(loop, inner + step)))
        else:
            for step, at, size, to in ((-2, 1, 3, 7), (-1, 0, 4, 3), (0, 0, 3, 0)):
                found.append(("site", at, size, "right", to, home(loop - 1, inner + step)))
        for slot, step in enumerate((1, 0, -1)):
            found.append(("notes", 0, 24, "meta", 24 * slot, home(loop, inner + step)))
    elif phase == 1 and bond % 2 == 0:
        for step, at, size, to in ((2, 1, 2, 1), (2, 3, 1, 6), (1, 0, 1, 0), (1, 1, 2, 4), (1, 3, 1, 9), (0, 0, 1, 3), (0, 1, 2, 7)):
            found.append(("new_right", at, size, "left", to, home(bond + 1, inner + step)))
    elif phase == 2 and bond % 2 == 0:
        for step in (0, 1, 2):
            found.append(("level", 0, 8, "levels", 8 * step, home(bond + 1, inner + step)))
        found.append(("level", 0, 8, "weights", 0, (bond, inner)))
        for step, at, size, to in ((-2, 1, 3, 7), (-1, 0, 4, 3), (0, 0, 3, 0)):
            found.append(("new_left", at, size, "right", to, home(bond - 1, inner + step)))
    elif phase == 2 and bond % 2 == 1:
        found.append(("level", 0, 8, "weights", 0, (bond, inner)))
        found.append(("new_left", 0, 4, "sites", 0, (bond, inner)))
        for step, at, size in ((2, 3, 1), (1, 1, 2), (0, 0, 1)):
            found.append(("new_right", at, size, "sites", at, (bond + 1, inner + step)))
    return [f[:5] + ((f[5][0] - loop, f[5][1] - inner),) for f in found]


def arrivals(phase, loop, inner):
    found = []
    for far in range(-3, 4):
        for away in range(-3, 4):
            for _, _, size, to, at, (x, y) in sends(phase, loop + far, inner + away):
                if (far + x, away + y) == (0, 0):
                    found.append((to, at, size, (far, away)))
    return found


def kind_of(kind):
    return (4 + kind // 2, 4 + kind % 2)


PHASES = (0, 1, 2)
LANDINGS = sorted({a[:3] for phase in PHASES for kind in range(4) for a in arrivals(phase, *kind_of(kind))})
MOST = max(sum(len(sends(phase, *kind_of(kind))) for phase in PHASES) for kind in range(4))


def partners(loop, inner):
    known = {s[5] for phase in PHASES for s in sends(phase, loop, inner)}
    known |= {a[3] for phase in PHASES for a in arrivals(phase, loop, inner)}
    return sorted(known - {(0, 0)})


def by_kind(work):
    loop, inner = lax.axis_index("loop"), lax.axis_index("inner")
    for kind in range(4):
        pl.when((lax.rem(loop, 2) == kind // 2) & (lax.rem(inner, 2) == kind % 2))(functools.partial(work, kind))


def device(offset):
    loop, inner = lax.axis_index("loop"), lax.axis_index("inner")
    rounds, sectors = lax.axis_size("loop"), lax.axis_size("inner")
    return (lax.rem(loop + offset[0] + rounds, rounds), lax.rem(inner + offset[1] + sectors, sectors))


def greet(barrier, kind):
    friends = partners(*kind_of(kind))
    for offset in friends:
        pl.semaphore_signal(barrier, inc=1, device_id=device(offset), device_id_type=MESH)
    pl.semaphore_wait(barrier, len(friends))


def outgoing(phase, refs, send_sems, recv_sems, kind):
    first = sum(len(sends(p, *kind_of(kind))) for p in range(phase))
    copies = []
    for n, (source, at, size, to, where, offset) in enumerate(sends(phase, *kind_of(kind))):
        src, dst = refs[source].at[pl.ds(at, size)], refs[to].at[pl.ds(where, size)]
        slot = recv_sems.at[LANDINGS.index((to, where, size))]
        if offset == (0, 0):
            copies.append((None, pltpu.make_async_copy(src, dst, slot)))
        else:
            sem = send_sems.at[first + n]
            copies.append((sem, pltpu.make_async_remote_copy(src, dst, sem, slot, device_id=device(offset), device_id_type=MESH)))
    return copies


def start(phase, refs, send_sems, recv_sems, kind):
    for _, copy in outgoing(phase, refs, send_sems, recv_sems, kind):
        copy.start()


def finish(refs, send_sems, recv_sems, kind):
    for phase in PHASES:
        for sem, copy in outgoing(phase, refs, send_sems, recv_sems, kind):
            if sem is not None:
                copy.wait_send()


def expect(buffers, refs, recv_sems, kind):
    for phase in PHASES:
        for to, where, size, _ in arrivals(phase, *kind_of(kind)):
            if to in buffers:
                dst = refs[to].at[pl.ds(where, size)]
                pltpu.make_async_copy(dst, dst, recv_sems.at[LANDINGS.index((to, where, size))]).wait()


def terms_of(outer_a, outer_b):
    found = []
    for d, a, b in PAIRS:
        if CHARGE[a] - CHARGE[outer_a] == d and CHARGE[outer_b] - CHARGE[b] == d:
            found.append(((outer_a * 4 + outer_b) * 16 + a * 4 + b, THETA_AT[d, a, b]))
    return found


def invert_leaf(work):
    n = 128
    lane = lax.broadcasted_iota(jnp.int32, (8, n), 1)
    sub = lax.broadcasted_iota(jnp.int32, (8, n), 0)
    tiles = [work[8 * t:8 * t + 8, :] for t in range(n // 8)]
    for g in range(n // 8):
        k = 8 * g
        cols = {}
        for t in range(g, n // 8):
            cols[t] = [jnp.broadcast_to(tiles[t][:, k + j:k + j + 1], (8, n)) for j in range(8)]
        fresh = (lane >= k) & (lane < k + 8)
        head = jnp.where(fresh, jnp.where(lane - k == sub, 1.0, 0.0), tiles[g])
        for t in range(g + 1, n // 8):
            tiles[t] = jnp.where(fresh, 0.0, tiles[t])
        rows = []
        for j in range(8):
            scale = lax.rsqrt(jnp.broadcast_to(cols[g][j][j:j + 1, :], (8, n)))
            for t in range(g, n // 8):
                cols[t][j] = cols[t][j] * scale
            low = jnp.where(sub > j, cols[g][j], 0.0)
            for i in range(j + 1, 8):
                other = jnp.broadcast_to(low[i:i + 1, :], (8, n))
                for t in range(g, n // 8):
                    cols[t][i] = cols[t][i] - (low if t == g else cols[t][j]) * other
            row = jnp.broadcast_to(head[j:j + 1, :], (8, n)) * scale
            rows.append(row)
            head = jnp.where(sub == j, row, head - low * row)
        for t in range(g + 1, n // 8):
            total = tiles[t]
            for j in range(8):
                total = total - cols[t][j] * rows[j]
            tiles[t] = total
        work[8 * g:8 * g + 8, :] = jnp.where(lane <= sub + k, head, 0.0)


def body(site, weights_in, gates_in, kept_in, sites, weights_out, left, right, meta, levels, weights, notes, new_left, new_right,
         level, theta, matrix, proj, gram, work, scaled, numbers, send_sems, recv_sems, sem):
    n = SLOTS
    refs = dict(site=site.at[0, 0], sites=sites.at[0, 0], left=left, right=right, meta=meta, levels=levels, weights=weights,
                notes=notes, new_left=new_left, new_right=new_right, level=level)
    state = (refs, send_sems, recv_sems)
    last = lax.rem(lax.axis_index("loop") + lax.axis_index("inner"), 2) == 0
    notes[0:8, :] = jnp.broadcast_to(weights_in[0], (8, n))
    gates = gates_in[0].astype(jnp.bfloat16).astype(jnp.float32)
    notes[8:24, :] = jnp.pad(gates, ((0, 0), (0, n - 16)))
    notes[7:8, :] = jnp.full((1, n), kept_in[0, 0].astype(jnp.float32))
    levels[...] = jnp.ones_like(levels)
    barrier = pltpu.get_barrier_semaphore()

    @by_kind
    def _(kind):
        greet(barrier, kind)
        start(0, *state, kind)
        expect(("meta",), refs, recv_sems, kind)
        expect(("left",), refs, recv_sems, kind)

    copy = pltpu.make_async_copy(meta.at[pl.ds(24, 24)], numbers, sem)
    copy.start()
    for d, at in LEFT_AT.items():
        row = meta[24 * (d + 1):24 * (d + 1) + 1, :]
        for k in at.values():
            scaled[k] = (left[k].astype(jnp.float32) * row).astype(jnp.bfloat16)

    @by_kind
    def _(kind):
        expect(("right",), refs, recv_sems, kind)

    for d, a, b in PAIRS:
        product = jnp.dot(scaled[LEFT_AT[d][a]], right[RIGHT_AT[d][b]], preferred_element_type=jnp.float32)
        theta[THETA_AT[d, a, b]] = (product * (1.0 / 16.0)).astype(jnp.bfloat16)
    copy.wait()

    @pl.loop(0, n // 16)
    def _(step):
        r = pl.multiple_of(step * 16, 16)
        for a in range(4):
            for b in range(4):
                total = None
                for g, t in terms_of(a, b):
                    term = theta[t, pl.ds(r, 16), :].astype(jnp.float32) * numbers[8 + g // 16, g % 16]
                    total = term if total is None else total + term
                matrix[pl.ds(pl.multiple_of(a * n + r, 16), 16), b * n:(b + 1) * n] = total.astype(jnp.bfloat16)

    down = lax.broadcasted_iota(jnp.int32, (n, n), 0)
    diagonal = down == lax.broadcasted_iota(jnp.int32, (n, n), 1)
    total = None
    for a in range(4):
        part = jnp.dot(left[3 + a].T, matrix[a * n:(a + 1) * n, :], preferred_element_type=jnp.float32)
        total = part if total is None else total + part
    row_number = lax.broadcasted_iota(jnp.int32, (n, 4 * n), 0).astype(jnp.float32)
    proj[...] = jnp.where(row_number < numbers[7, 0], total, 0.0)
    dot = functools.partial(lax.dot_general, precision=HI, preferred_element_type=jnp.float32)
    gram[...] = dot(proj[...], proj[...], NT) + jnp.where(diagonal, 1.0, 0.0)
    h = n // 2
    work[...] = gram[:h, :h]
    invert_leaf(work)
    first = work[...]
    lower = dot(gram[h:, :h], first, NT)
    top = dot(first, proj[:h, :], NN)
    work[...] = gram[h:, h:] - dot(lower, lower, NT)
    proj[h:, :] = proj[h:, :] - dot(lower, top, NN)
    proj[:h, :] = top
    invert_leaf(work)
    proj[h:, :] = dot(work[...], proj[h:, :], NN)
    iso = (proj[...] * 32.0).astype(jnp.bfloat16)
    for a in range(4):
        new_right[a] = iso[:, a * n:(a + 1) * n]

    @by_kind
    def _(kind):
        start(1, *state, kind)

    carried = []
    squares = jnp.zeros((1, n), jnp.float32)
    for a in range(4):
        part = lax.dot_general(matrix[a * n:(a + 1) * n, :], iso, NT, preferred_element_type=jnp.float32) * (1.0 / 32.0)
        carried.append(part)
        squares = squares + jnp.sum(part * part, axis=0, keepdims=True)
    lev = jnp.sqrt(squares * (1.0 / 1024.0) + 1e-6)
    level[...] = jnp.broadcast_to(lev, (8, n))

    def upright(row):
        return jnp.sum(jnp.where(diagonal, row, 0.0), axis=1, keepdims=True)

    @by_kind
    def _(kind):
        expect(("levels",), refs, recv_sems, kind)

    for a in range(4):
        block = (carried[a] / lev).astype(jnp.bfloat16).astype(jnp.float32)
        new_left[a] = (block * upright(levels[8 * CHARGE[a]:8 * CHARGE[a] + 1, :])).astype(jnp.bfloat16)

    @pl.when(last)
    def _():
        scale = upright(lev)
        for a in range(4):
            new_right[a] = (new_right[a].astype(jnp.float32) * scale).astype(jnp.bfloat16)

    @by_kind
    def _(kind):
        start(2, *state, kind)
        expect(("weights", "sites"), refs, recv_sems, kind)
        finish(*state, kind)

    weights_out[0] = weights[0:1, :]


def per_device(site_blocks, bond_weights, bond_gates, kept_slots):
    n = SLOTS
    vmem = pl.BlockSpec(memory_space=pltpu.VMEM)
    blocks = lambda count: pltpu.VMEM((count, n, n), jnp.bfloat16)
    rows = lambda count: pltpu.VMEM((count, n), jnp.float32)
    return pl.pallas_call(
        body,
        out_shape=(
            jax.ShapeDtypeStruct(site_blocks.shape, jnp.bfloat16),
            jax.ShapeDtypeStruct(bond_weights.shape, jnp.float32),
        ),
        in_specs=[pl.BlockSpec(memory_space=pl.ANY), vmem, vmem, pl.BlockSpec(memory_space=pltpu.SMEM)],
        out_specs=(pl.BlockSpec(memory_space=pl.ANY), vmem),
        scratch_shapes=[
            blocks(10), blocks(10), rows(72), rows(24), rows(8), rows(24), blocks(4), blocks(4), rows(8),
            blocks(len(PAIRS)),
            pltpu.VMEM((4 * n, 4 * n), jnp.bfloat16),
            pltpu.VMEM((n, 4 * n), jnp.float32),
            pltpu.VMEM((n, n), jnp.float32),
            pltpu.VMEM((n // 2, n // 2), jnp.float32),
            blocks(10),
            pltpu.SMEM((24, n), jnp.float32),
            pltpu.SemaphoreType.DMA((MOST,)),
            pltpu.SemaphoreType.DMA((len(LANDINGS),)),
            pltpu.SemaphoreType.DMA,
        ],
        compiler_params=pltpu.CompilerParams(collective_id=0, has_side_effects=True, vmem_limit_bytes=40 << 20),
    )(site_blocks, bond_weights, bond_gates, kept_slots)


def solution(mesh):
    return jax.shard_map(
        per_device,
        mesh=mesh,
        in_specs=(
            P("loop", "inner", None, None, None),
            P("loop", "inner", None),
            P("loop", None, None),
            P("loop", "inner"),
        ),
        out_specs=(P("loop", "inner", None, None, None), P("loop", "inner", None)),
        check_vma=False,
    )
```

time: 120 us -> 96.8 us (0.81)
  the two profiles are of different devices: /device:TPU:7 before, /device:TPU:1 now
where the time goes in v1:
time: 96.8 us; the launch traced here: 95.5 us
  Pallas kernels  91 us (94%)
  local copies, waits for them, and re-layouts  3.1 us (3%)
  between operations  1.31 us (1%)
    pallas_call x1, Pallas kernels, per_device(): pl.pallas_call(body, out_shape=(jax.ShapeDtypeStruct(site_blocks.shape, j...  91 us
    unnamed x8, local copies, waits for them, and re-layouts  3.1 us

profile of v1, /device:TPU:1, one launch (start us, length us, event | category | flops | bytes accessed | tf_op | source)
XLA Modules:
  0.0 95.5 jit_solution(2186525873707119315)
XLA Ops:
  0.6 0.0 copy-start.2
  1.3 0.0 copy-done.2
  1.3 0.0 copy-start
  1.3 1.0 %copy-done = bf16[1,1,4,256,256]{4,3,2,1,0:T(8,128)(2,1)S(1)} copy-done((bf16[1,1,4,256,256]{4,3,2,1,0:T(8,128)(2,1)S(1)}, bf16[1,1,4,256,256]{4,3,2,1,0:T(8,128)(2,1)}, u32[]{:S(2)}) %copy-start) | copy-done | bytes 524312
  2.4 0.0 copy-start.1
  2.4 0.7 copy-done.1
  3.0 91.0 %shard_map.59 = (bf16[1,1,4,256,256]{4,3,2,1,0:T(8,128)(2,1)S(1)}, f32[1,1,256]{2,1,0:T(1,128)S(1)}) custom-call(bf16[1,1,4,256,256]{4,3,2,1,0:T(8,128)(2,1)S(1)} %copy-done, f32[1,1,256]{2,1,0:T(1,128)S(1)} %copy-done.2, f32[1,16,16]{2,1,0:T(8,128)S(1)} %copy-done.1, s32[1,1]{1,0:T(1,128)S(6)} %copy.8.kept_in), custom_call_target="tpu_custom_call" | custom-call | tf_op jit(solution)/shard_map/pallas_call | solution.py:295
  94.1 0.8 copy.9
  94.9 0.6 copy.10
Async XLA Ops:
  0.6 0.7 copy-start.2
  1.3 1.0 %copy-start = (bf16[1,1,4,256,256]{4,3,2,1,0:T(8,128)(2,1)S(1)}, bf16[1,1,4,256,256]{4,3,2,1,0:T(8,128)(2,1)}, u32[]{:S(2)}) copy-start(bf16[1,1,4,256,256]{4,3,2,1,0:T(8,128)(2,1)} %site.1) | copy-start | bytes 1572868
  2.4 0.7 copy-start.1

commit v2 on v1

v2 whole, which is shorter than its diff:
```python
import functools

import jax
import jax.numpy as jnp
from jax import lax
from jax.experimental import pallas as pl
from jax.experimental.pallas import tpu as pltpu
from jax.sharding import PartitionSpec as P

HI = lax.Precision.HIGHEST
NN = (((1,), (0,)), ((), ()))
NT = (((1,), (1,)), ((), ()))
MESH = pl.DeviceIdType.MESH
SLOTS = 256
CHARGE = (0, 1, 1, 2)

LEFT_AT = {-1: {0: 0, 1: 1, 2: 2}, 0: {0: 3, 1: 4, 2: 5, 3: 6}, 1: {1: 7, 2: 8, 3: 9}}
RIGHT_AT = {-1: {1: 1, 2: 2, 3: 6}, 0: {0: 0, 1: 4, 2: 5, 3: 9}, 1: {0: 3, 1: 7, 2: 8}}
PAIRS = [(d, a, b) for d in (-1, 0, 1) for a in LEFT_AT[d] for b in RIGHT_AT[d]]
THETA_AT = {key: n for n, key in enumerate(PAIRS)}


def even(number):
    return 1 - number % 2


def sends(phase, loop, inner):
    home = lambda bond, sector: (bond + even(sector), sector)
    bond = loop - even(inner)
    found = []
    if phase == 0:
        if loop % 2 == 0:
            for step, at, size, to in ((-1, 1, 3, 7), (1, 0, 3, 0), (0, 0, 4, 3)):
                found.append(("site", at, size, "left", to, None, home(loop, inner + step)))
        else:
            for step, at, size, to in ((-2, 1, 3, 7), (-1, 0, 4, 3), (0, 0, 3, 0)):
                found.append(("site", at, size, "right", to, None, home(loop - 1, inner + step)))
        for slot, step in enumerate((1, 0, -1)):
            found.append(("notes", 0, 24, "meta", 24 * slot, None, home(loop, inner + step)))
    elif bond % 2 == 0:
        half = (phase - 1) // 2
        if phase % 2 == 1:
            for step, at, size, to in ((2, 1, 2, 1), (2, 3, 1, 6), (1, 0, 1, 0), (1, 1, 2, 4), (1, 3, 1, 9), (0, 0, 1, 3), (0, 1, 2, 7)):
                found.append(("new_right", at, size, "left", to, half, home(bond + 1, inner + step)))
        else:
            if half == 1:
                for step in (0, 1, 2):
                    found.append(("level", 0, 8, "levels", 8 * step, None, home(bond + 1, inner + step)))
                found.append(("level", 0, 8, "weights", 0, None, (bond, inner)))
            for step, at, size, to in ((-2, 1, 3, 7), (-1, 0, 4, 3), (0, 0, 3, 0)):
                found.append(("new_left", at, size, "right", to, half, home(bond - 1, inner + step)))
    elif phase % 2 == 0:
        half = (phase - 1) // 2
        if half == 1:
            found.append(("level", 0, 8, "weights", 0, None, (bond, inner)))
        found.append(("new_left", 0, 4, "sites", 0, half, (bond, inner)))
        for step, at, size in ((2, 3, 1), (1, 1, 2), (0, 0, 1)):
            found.append(("new_right", at, size, "sites", at, half, (bond + 1, inner + step)))
    return [f[:6] + ((f[6][0] - loop, f[6][1] - inner),) for f in found]


def spot_of(source, size, to, where, half):
    return (to, where, size, -1 if half is None else half, source == "new_right")


def part(ref, at, size, source, half):
    if half is None:
        return ref.at[pl.ds(at, size)]
    span = pl.ds(half * (SLOTS // 2), SLOTS // 2)
    return ref.at[pl.ds(at, size), span, :] if source == "new_right" else ref.at[pl.ds(at, size), :, span]


def arrivals(phase, loop, inner):
    found = []
    for far in range(-3, 4):
        for away in range(-3, 4):
            for source, _, size, to, at, half, (x, y) in sends(phase, loop + far, inner + away):
                if (far + x, away + y) == (0, 0):
                    found.append((source, to, at, size, half, (far, away)))
    return found


def kind_of(kind):
    return (4 + kind // 2, 4 + kind % 2)


PHASES = (0, 1, 2, 3, 4)
LANDINGS = sorted({spot_of(a[0], a[3], a[1], a[2], a[4]) for phase in PHASES for kind in range(4) for a in arrivals(phase, *kind_of(kind))})
MOST = max(sum(len(sends(phase, *kind_of(kind))) for phase in PHASES) for kind in range(4))


def partners(loop, inner):
    known = {s[6] for phase in PHASES for s in sends(phase, loop, inner)}
    known |= {a[5] for phase in PHASES for a in arrivals(phase, loop, inner)}
    return sorted(known - {(0, 0)})


def by_kind(work):
    loop, inner = lax.axis_index("loop"), lax.axis_index("inner")
    for kind in range(4):
        pl.when((lax.rem(loop, 2) == kind // 2) & (lax.rem(inner, 2) == kind % 2))(functools.partial(work, kind))


def device(offset):
    loop, inner = lax.axis_index("loop"), lax.axis_index("inner")
    rounds, sectors = lax.axis_size("loop"), lax.axis_size("inner")
    return (lax.rem(loop + offset[0] + rounds, rounds), lax.rem(inner + offset[1] + sectors, sectors))


def greet(barrier, kind):
    friends = partners(*kind_of(kind))
    for offset in friends:
        pl.semaphore_signal(barrier, inc=1, device_id=device(offset), device_id_type=MESH)
    pl.semaphore_wait(barrier, len(friends))


def outgoing(phase, refs, send_sems, recv_sems, kind):
    first = sum(len(sends(p, *kind_of(kind))) for p in range(phase))
    for n, (source, at, size, to, where, half, offset) in enumerate(sends(phase, *kind_of(kind))):
        src, dst = part(refs[source], at, size, source, half), part(refs[to], where, size, source, half)
        slot = recv_sems.at[LANDINGS.index(spot_of(source, size, to, where, half))]
        sem = send_sems.at[first + n]
        yield src, dst, sem, slot, offset


def start(phase, refs, send_sems, recv_sems, kind):
    for src, dst, sem, slot, offset in outgoing(phase, refs, send_sems, recv_sems, kind):
        if offset == (0, 0):
            pltpu.make_async_copy(src, dst, slot).start()
        else:
            pltpu.make_async_remote_copy(src, dst, sem, slot, device_id=device(offset), device_id_type=MESH).start()


def finish(refs, send_sems, recv_sems, kind):
    for phase in PHASES:
        for src, dst, sem, slot, offset in outgoing(phase, refs, send_sems, recv_sems, kind):
            if offset != (0, 0):
                pltpu.make_async_remote_copy(src, dst, sem, slot, device_id=device(offset), device_id_type=MESH).wait_send()


def expect(buffers, refs, recv_sems, kind, halves=(None, 0, 1)):
    for phase in PHASES:
        for source, to, where, size, half, _ in arrivals(phase, *kind_of(kind)):
            if to in buffers and half in halves:
                dst = part(refs[to], where, size, source, half)
                pltpu.make_async_copy(dst, dst, recv_sems.at[LANDINGS.index(spot_of(source, size, to, where, half))]).wait()


def terms_of(outer_a, outer_b):
    found = []
    for d, a, b in PAIRS:
        if CHARGE[a] - CHARGE[outer_a] == d and CHARGE[outer_b] - CHARGE[b] == d:
            found.append(((outer_a * 4 + outer_b) * 16 + a * 4 + b, THETA_AT[d, a, b]))
    return found


def invert_leaf(work):
    n = 128
    lane = lax.broadcasted_iota(jnp.int32, (8, n), 1)
    sub = lax.broadcasted_iota(jnp.int32, (8, n), 0)
    tiles = [work[8 * t:8 * t + 8, :] for t in range(n // 8)]
    for g in range(n // 8):
        k = 8 * g
        cols = {}
        for t in range(g, n // 8):
            cols[t] = [jnp.broadcast_to(tiles[t][:, k + j:k + j + 1], (8, n)) for j in range(8)]
        fresh = (lane >= k) & (lane < k + 8)
        head = jnp.where(fresh, jnp.where(lane - k == sub, 1.0, 0.0), tiles[g])
        for t in range(g + 1, n // 8):
            tiles[t] = jnp.where(fresh, 0.0, tiles[t])
        rows = []
        for j in range(8):
            scale = lax.rsqrt(jnp.broadcast_to(cols[g][j][j:j + 1, :], (8, n)))
            for t in range(g, n // 8):
                cols[t][j] = cols[t][j] * scale
            low = jnp.where(sub > j, cols[g][j], 0.0)
            for i in range(j + 1, 8):
                other = jnp.broadcast_to(low[i:i + 1, :], (8, n))
                for t in range(g, n // 8):
                    cols[t][i] = cols[t][i] - (low if t == g else cols[t][j]) * other
            row = jnp.broadcast_to(head[j:j + 1, :], (8, n)) * scale
            rows.append(row)
            head = jnp.where(sub == j, row, head - low * row)
        for t in range(g + 1, n // 8):
            total = tiles[t]
            for j in range(8):
                total = total - cols[t][j] * rows[j]
            tiles[t] = total
        work[8 * g:8 * g + 8, :] = jnp.where(lane <= sub + k, head, 0.0)


def body(site, weights_in, gates_in, kept_in, sites, weights_out, left, right, meta, levels, weights, notes, new_left, new_right,
         level, theta, matrix, proj, gram, work, scaled, numbers, lines, table, send_sems, recv_sems, sems):
    n = SLOTS
    h = n // 2
    refs = dict(site=site.at[0, 0], sites=sites.at[0, 0], left=left, right=right, meta=meta, levels=levels, weights=weights,
                notes=notes, new_left=new_left, new_right=new_right, level=level)
    state = (refs, send_sems, recv_sems)
    last = lax.rem(lax.axis_index("loop") + lax.axis_index("inner"), 2) == 0
    small = [
        pltpu.make_async_copy(weights_in.at[0], lines, sems.at[0]),
        pltpu.make_async_copy(gates_in.at[0], table, sems.at[1]),
    ]
    for copy in small:
        copy.start()
    levels[...] = jnp.ones_like(levels)
    barrier = pltpu.get_barrier_semaphore()

    @by_kind
    def _(kind):
        for offset in partners(*kind_of(kind)):
            pl.semaphore_signal(barrier, inc=1, device_id=device(offset), device_id_type=MESH)

    for copy in small:
        copy.wait()
    notes[0:7, :] = jnp.broadcast_to(lines[...], (7, n))
    notes[7:8, :] = jnp.full((1, n), kept_in[0, 0].astype(jnp.float32))
    notes[8:24, :] = jnp.pad(table[...].astype(jnp.bfloat16).astype(jnp.float32), ((0, 0), (0, n - 16)))

    @by_kind
    def _(kind):
        pl.semaphore_wait(barrier, len(partners(*kind_of(kind))))
        start(0, *state, kind)
        expect(("meta",), refs, recv_sems, kind)

    copy = pltpu.make_async_copy(meta.at[pl.ds(24, 24)], numbers, sems.at[2])
    copy.start()

    @by_kind
    def _(kind):
        expect(("left",), refs, recv_sems, kind)

    for d, at in LEFT_AT.items():
        row = meta[24 * (d + 1):24 * (d + 1) + 1, :]
        for k in at.values():
            scaled[k] = (left[k].astype(jnp.float32) * row).astype(jnp.bfloat16)

    @by_kind
    def _(kind):
        expect(("right", "levels"), refs, recv_sems, kind)

    for d, a, b in PAIRS:
        product = jnp.dot(scaled[LEFT_AT[d][a]], right[RIGHT_AT[d][b]], preferred_element_type=jnp.float32)
        theta[THETA_AT[d, a, b]] = (product * (1.0 / 16.0)).astype(jnp.bfloat16)
    copy.wait()

    @pl.loop(0, n // 16)
    def _(step):
        r = pl.multiple_of(step * 16, 16)
        for a in range(4):
            for b in range(4):
                total = None
                for g, t in terms_of(a, b):
                    term = theta[t, pl.ds(r, 16), :].astype(jnp.float32) * numbers[8 + g // 16, g % 16]
                    total = term if total is None else total + term
                matrix[pl.ds(pl.multiple_of(a * n + r, 16), 16), b * n:(b + 1) * n] = total.astype(jnp.bfloat16)

    total = None
    for a in range(4):
        product = jnp.dot(left[3 + a].T, matrix[a * n:(a + 1) * n, :], preferred_element_type=jnp.float32)
        total = product if total is None else total + product
    row_number = lax.broadcasted_iota(jnp.int32, (n, 4 * n), 0).astype(jnp.float32)
    proj[...] = jnp.where(row_number < numbers[7, 0], total, 0.0)
    dot = functools.partial(lax.dot_general, precision=HI, preferred_element_type=jnp.float32)
    diagonal = lambda size: lax.broadcasted_iota(jnp.int32, (size, size), 0) == lax.broadcasted_iota(jnp.int32, (size, size), 1)
    upright = lambda row: jnp.sum(jnp.where(diagonal(row.shape[1]), row, 0.0), axis=1, keepdims=True)
    gram[...] = dot(proj[...], proj[...], NT) + jnp.where(diagonal(n), 1.0, 0.0)

    def right_half(half, ortho):
        iso = (ortho * 32.0).astype(jnp.bfloat16)
        for a in range(4):
            new_right[a, half * h:(half + 1) * h, :] = iso[:, a * n:(a + 1) * n]

        @by_kind
        def _(kind):
            start(1 + 2 * half, *state, kind)

        return iso

    def left_half(half, iso):
        span = slice(half * h, (half + 1) * h)
        carried = []
        squares = jnp.zeros((1, h), jnp.float32)
        for a in range(4):
            product = lax.dot_general(matrix[a * n:(a + 1) * n, :], iso, NT, preferred_element_type=jnp.float32) * (1.0 / 32.0)
            carried.append(product)
            squares = squares + jnp.sum(product * product, axis=0, keepdims=True)
        lev = jnp.sqrt(squares * (1.0 / 1024.0) + 1e-6)
        level[:, span] = jnp.broadcast_to(lev, (8, h))
        inverse = 1.0 / lev
        for a in range(4):
            block = (carried[a] * inverse).astype(jnp.bfloat16).astype(jnp.float32)
            new_left[a, :, span] = (block * upright(levels[8 * CHARGE[a]:8 * CHARGE[a] + 1, :])).astype(jnp.bfloat16)

        @pl.when(last)
        def _():
            scale = upright(lev)
            for a in range(4):
                new_right[a, span, :] = (new_right[a, span, :].astype(jnp.float32) * scale).astype(jnp.bfloat16)

        @by_kind
        def _(kind):
            start(2 + 2 * half, *state, kind)

    work[...] = gram[:h, :h]
    invert_leaf(work)
    first = work[...]
    top = dot(first, proj[:h, :], NN)
    top_iso = right_half(0, top)
    lower = dot(gram[h:, :h], first, NT)
    work[...] = gram[h:, h:] - dot(lower, lower, NT)
    proj[h:, :] = proj[h:, :] - dot(lower, top, NN)
    left_half(0, top_iso)
    invert_leaf(work)
    left_half(1, right_half(1, dot(work[...], proj[h:, :], NN)))

    @by_kind
    def _(kind):
        expect(("weights", "sites"), refs, recv_sems, kind)
        finish(*state, kind)

    weights_out[0] = weights[0:1, :]


def per_device(site_blocks, bond_weights, bond_gates, kept_slots):
    n = SLOTS
    vmem = pl.BlockSpec(memory_space=pltpu.VMEM)
    blocks = lambda count: pltpu.VMEM((count, n, n), jnp.bfloat16)
    rows = lambda count: pltpu.VMEM((count, n), jnp.float32)
    return pl.pallas_call(
        body,
        out_shape=(
            jax.ShapeDtypeStruct(site_blocks.shape, jnp.bfloat16),
            jax.ShapeDtypeStruct(bond_weights.shape, jnp.float32),
        ),
        in_specs=[pl.BlockSpec(memory_space=pltpu.HBM)] * 3 + [pl.BlockSpec(memory_space=pltpu.SMEM)],
        out_specs=(pl.BlockSpec(memory_space=pl.ANY), vmem),
        scratch_shapes=[
            blocks(10), blocks(10), rows(72), rows(24), rows(8), rows(24), blocks(4), blocks(4), rows(8),
            blocks(len(PAIRS)),
            pltpu.VMEM((4 * n, 4 * n), jnp.bfloat16),
            pltpu.VMEM((n, 4 * n), jnp.float32),
            pltpu.VMEM((n, n), jnp.float32),
            pltpu.VMEM((n // 2, n // 2), jnp.float32),
            blocks(10),
            pltpu.SMEM((24, n), jnp.float32),
            rows(1),
            pltpu.VMEM((16, 16), jnp.float32),
            pltpu.SemaphoreType.DMA((MOST,)),
            pltpu.SemaphoreType.DMA((len(LANDINGS),)),
            pltpu.SemaphoreType.DMA((3,)),
        ],
        compiler_params=pltpu.CompilerParams(collective_id=0, has_side_effects=True, vmem_limit_bytes=40 << 20),
    )(*[pltpu.with_memory_space_constraint(x, pltpu.HBM) for x in (site_blocks, bond_weights, bond_gates)], kept_slots)


def solution(mesh):
    return jax.shard_map(
        per_device,
        mesh=mesh,
        in_specs=(
            P("loop", "inner", None, None, None),
            P("loop", "inner", None),
            P("loop", None, None),
            P("loop", "inner"),
        ),
        out_specs=(P("loop", "inner", None, None, None), P("loop", "inner", None)),
        check_vma=False,
    )
```

time: 96.8 us -> 87.6 us (0.905); the launches traced: 95.5 us -> 87.4 us
  Pallas kernels: 91 us -> 84.8 us
  local copies, waits for them, and re-layouts: 3.1 us -> 1.36 us
    pallas_call x1, Pallas kernels: 91 us -> 84.8 us  [per_device(): pl.pallas_call(body, out_shape=(jax.ShapeDtypeStruct(site_blocks.shape, j...]
    unnamed x8 -> x2, local copies, waits for them, and re-layouts: 3.1 us -> 1.36 us
where the time goes in v2:
time: 87.6 us; the launch traced here: 87.4 us
  Pallas kernels  84.8 us (97%)
  local copies, waits for them, and re-layouts  1.36 us (2%)
  between operations  1.29 us (1%)
    pallas_call x1, Pallas kernels, per_device(): pl.pallas_call(body, out_shape=(jax.ShapeDtypeStruct(site_blocks.shape, j...  84.8 us

profile of v2, /device:TPU:1, one launch (start us, length us, event | category | flops | bytes accessed | tf_op | source)
XLA Modules:
  0.0 87.4 jit_solution(10137671573060681286)
XLA Ops:
  1.3 84.8 %shard_map.59 = (bf16[1,1,4,256,256]{4,3,2,1,0:T(8,128)(2,1)S(1)}, f32[1,1,256]{2,1,0:T(1,128)S(1)}) custom-call(bf16[1,1,4,256,256]{4,3,2,1,0:T(8,128)(2,1)} %site.1, f32[1,1,256]{2,1,0:T(1,128)} %weights_in.1, f32[1,16,16]{2,1,0:T(8,128)} %gates_in.1, s32[1,1]{1,0:T(1,128)S(6)} %copy.8.kept_in), custom_call_target="tpu_custom_call" | custom-call | tf_op jit(solution)/shard_map/pallas_call | solution.py:330
  86.1 0.8 copy.9
  86.9 0.6 copy.10

commit v3 on v2

--- a/solution.py
+++ b/solution.py
@@ -90,8 +90,7 @@
 
 
 def partners(loop, inner):
-    known = {s[6] for phase in PHASES for s in sends(phase, loop, inner)}
-    known |= {a[5] for phase in PHASES for a in arrivals(phase, loop, inner)}
+    known = {s[6] for s in sends(0, loop, inner)} | {a[5] for a in arrivals(0, loop, inner)}
     return sorted(known - {(0, 0)})
 
 
@@ -105,13 +104,6 @@
     loop, inner = lax.axis_index("loop"), lax.axis_index("inner")
     rounds, sectors = lax.axis_size("loop"), lax.axis_size("inner")
     return (lax.rem(loop + offset[0] + rounds, rounds), lax.rem(inner + offset[1] + sectors, sectors))
-
-
-def greet(barrier, kind):
-    friends = partners(*kind_of(kind))
-    for offset in friends:
-        pl.semaphore_signal(barrier, inc=1, device_id=device(offset), device_id_type=MESH)
-    pl.semaphore_wait(barrier, len(friends))
 
 
 def outgoing(phase, refs, send_sems, recv_sems, kind):
@@ -170,17 +162,19 @@
             tiles[t] = jnp.where(fresh, 0.0, tiles[t])
         rows = []
         for j in range(8):
-            scale = lax.rsqrt(jnp.broadcast_to(cols[g][j][j:j + 1, :], (8, n)))
+            raw = [jnp.broadcast_to(cols[g][j][i:i + 1, :], (8, n)) for i in range(j, 8)]
+            scale = lax.rsqrt(raw[0])
             for t in range(g, n // 8):
                 cols[t][j] = cols[t][j] * scale
             low = jnp.where(sub > j, cols[g][j], 0.0)
             for i in range(j + 1, 8):
-                other = jnp.broadcast_to(low[i:i + 1, :], (8, n))
+                other = raw[i - j] * scale
                 for t in range(g, n // 8):
-                    cols[t][i] = cols[t][i] - (low if t == g else cols[t][j]) * other
+                    cols[t][i] = cols[t][i] - cols[t][j] * other
             row = jnp.broadcast_to(head[j:j + 1, :], (8, n)) * scale
             rows.append(row)
             head = jnp.where(sub == j, row, head - low * row)
+        tiles[g] = head
         for t in range(g + 1, n // 8):
             total = tiles[t]
             for j in range(8):
@@ -190,7 +184,7 @@
 
 
 def body(site, weights_in, gates_in, kept_in, sites, weights_out, left, right, meta, levels, weights, notes, new_left, new_right,
-         level, theta, matrix, proj, gram, work, scaled, numbers, lines, table, send_sems, recv_sems, sems):
+         level, theta, turned, matrix, proj, gram, work, scaled, numbers, lines, table, send_sems, recv_sems, sems):
     n = SLOTS
     h = n // 2
     refs = dict(site=site.at[0, 0], sites=sites.at[0, 0], left=left, right=right, meta=meta, levels=levels, weights=weights,
@@ -235,14 +229,22 @@
         for k in at.values():
             scaled[k] = (left[k].astype(jnp.float32) * row).astype(jnp.bfloat16)
 
-    @by_kind
-    def _(kind):
-        expect(("right", "levels"), refs, recv_sems, kind)
-
-    for d, a, b in PAIRS:
-        product = jnp.dot(scaled[LEFT_AT[d][a]], right[RIGHT_AT[d][b]], preferred_element_type=jnp.float32)
-        theta[THETA_AT[d, a, b]] = (product * (1.0 / 16.0)).astype(jnp.bfloat16)
+    for a in range(4):
+        turned[a] = left[3 + a].T
     copy.wait()
+
+    for side in range(2):
+
+        @by_kind
+        def _(kind):
+            expect(("right",), refs, recv_sems, kind, (None, 0) if side == 0 else (1,))
+
+        for d in LEFT_AT:
+            wide = jnp.concatenate([right[k, :, side * h:(side + 1) * h] for k in RIGHT_AT[d].values()], axis=1)
+            for a, k in LEFT_AT[d].items():
+                product = (jnp.dot(scaled[k], wide, preferred_element_type=jnp.float32) * (1.0 / 16.0)).astype(jnp.bfloat16)
+                for i, b in enumerate(RIGHT_AT[d]):
+                    theta[THETA_AT[d, a, b], :, side * h:(side + 1) * h] = product[:, i * h:(i + 1) * h]
 
     @pl.loop(0, n // 16)
     def _(step):
@@ -257,7 +259,7 @@
 
     total = None
     for a in range(4):
-        product = jnp.dot(left[3 + a].T, matrix[a * n:(a + 1) * n, :], preferred_element_type=jnp.float32)
+        product = jnp.dot(turned[a], matrix[a * n:(a + 1) * n, :], preferred_element_type=jnp.float32)
         total = product if total is None else total + product
     row_number = lax.broadcasted_iota(jnp.int32, (n, 4 * n), 0).astype(jnp.float32)
     proj[...] = jnp.where(row_number < numbers[7, 0], total, 0.0)
@@ -301,6 +303,10 @@
         @by_kind
         def _(kind):
             start(2 + 2 * half, *state, kind)
+
+    @by_kind
+    def _(kind):
+        expect(("levels",), refs, recv_sems, kind)
 
     work[...] = gram[:h, :h]
     invert_leaf(work)
@@ -338,6 +344,7 @@
         scratch_shapes=[
             blocks(10), blocks(10), rows(72), rows(24), rows(8), rows(24), blocks(4), blocks(4), rows(8),
             blocks(len(PAIRS)),
+            blocks(4),
             pltpu.VMEM((4 * n, 4 * n), jnp.bfloat16),
             pltpu.VMEM((n, 4 * n), jnp.float32),
             pltpu.VMEM((n, n), jnp.float32),

time: 87.6 us -> 84.9 us (0.969)
  Pallas kernels: 84.8 us -> 82.1 us
    pallas_call x1, Pallas kernels: 84.8 us -> 82.1 us  [per_device(): pl.pallas_call(body, out_shape=(jax.ShapeDtypeStruct(site_blocks.shape, j...]
where the time goes in v3:
time: 84.9 us; the launch traced here: 84.7 us
  Pallas kernels  82.1 us (97%)
  local copies, waits for them, and re-layouts  1.36 us (2%)
  between operations  1.29 us (2%)
    pallas_call x1, Pallas kernels, per_device(): pl.pallas_call(body, out_shape=(jax.ShapeDtypeStruct(site_blocks.shape, j...  82.1 us

profile of v3, /device:TPU:1, one launch (start us, length us, event | category | flops | bytes accessed | tf_op | source)
XLA Modules:
  0.0 84.7 jit_solution(14667394327410365789)
XLA Ops:
  1.3 82.1 %shard_map.59 = (bf16[1,1,4,256,256]{4,3,2,1,0:T(8,128)(2,1)S(1)}, f32[1,1,256]{2,1,0:T(1,128)S(1)}) custom-call(bf16[1,1,4,256,256]{4,3,2,1,0:T(8,128)(2,1)} %site.1, f32[1,1,256]{2,1,0:T(1,128)} %weights_in.1, f32[1,16,16]{2,1,0:T(8,128)} %gates_in.1, s32[1,1]{1,0:T(1,128)S(6)} %copy.8.kept_in), custom_call_target="tpu_custom_call" | custom-call | tf_op jit(solution)/shard_map/pallas_call | solution.py:336
  83.4 0.8 copy.9
  84.2 0.6 copy.10

commit v4 on v3

--- a/solution.py
+++ b/solution.py
@@ -33,8 +33,9 @@
             for step, at, size, to in ((-1, 1, 3, 7), (1, 0, 3, 0), (0, 0, 4, 3)):
                 found.append(("site", at, size, "left", to, None, home(loop, inner + step)))
         else:
-            for step, at, size, to in ((-2, 1, 3, 7), (-1, 0, 4, 3), (0, 0, 3, 0)):
-                found.append(("site", at, size, "right", to, None, home(loop - 1, inner + step)))
+            for half in (0, 1):
+                for step, at, size, to in ((-2, 1, 3, 7), (-1, 0, 4, 3), (0, 0, 3, 0)):
+                    found.append(("site", at, size, "right", to, half, home(loop - 1, inner + step)))
         for slot, step in enumerate((1, 0, -1)):
             found.append(("notes", 0, 24, "meta", 24 * slot, None, home(loop, inner + step)))
     elif bond % 2 == 0:
@@ -63,9 +64,12 @@
     return (to, where, size, -1 if half is None else half, source == "new_right")
 
 
-def part(ref, at, size, source, half):
+def part(refs, name, at, size, source, half):
+    ref = refs[name]
     if half is None:
         return ref.at[pl.ds(at, size)]
+    if name in ("new_left", "right"):
+        return ref.at[half, pl.ds(at, size)]
     span = pl.ds(half * (SLOTS // 2), SLOTS // 2)
     return ref.at[pl.ds(at, size), span, :] if source == "new_right" else ref.at[pl.ds(at, size), :, span]
 
@@ -109,7 +113,7 @@
 def outgoing(phase, refs, send_sems, recv_sems, kind):
     first = sum(len(sends(p, *kind_of(kind))) for p in range(phase))
     for n, (source, at, size, to, where, half, offset) in enumerate(sends(phase, *kind_of(kind))):
-        src, dst = part(refs[source], at, size, source, half), part(refs[to], where, size, source, half)
+        src, dst = part(refs, source, at, size, source, half), part(refs, to, where, size, source, half)
         slot = recv_sems.at[LANDINGS.index(spot_of(source, size, to, where, half))]
         sem = send_sems.at[first + n]
         yield src, dst, sem, slot, offset
@@ -134,7 +138,7 @@
     for phase in PHASES:
         for source, to, where, size, half, _ in arrivals(phase, *kind_of(kind)):
             if to in buffers and half in halves:
-                dst = part(refs[to], where, size, source, half)
+                dst = part(refs, to, where, size, source, half)
                 pltpu.make_async_copy(dst, dst, recv_sems.at[LANDINGS.index(spot_of(source, size, to, where, half))]).wait()
 
 
@@ -237,10 +241,10 @@
 
         @by_kind
         def _(kind):
-            expect(("right",), refs, recv_sems, kind, (None, 0) if side == 0 else (1,))
+            expect(("right",), refs, recv_sems, kind, (side,))
 
         for d in LEFT_AT:
-            wide = jnp.concatenate([right[k, :, side * h:(side + 1) * h] for k in RIGHT_AT[d].values()], axis=1)
+            wide = jnp.concatenate([right[side, k] for k in RIGHT_AT[d].values()], axis=1)
             for a, k in LEFT_AT[d].items():
                 product = (jnp.dot(scaled[k], wide, preferred_element_type=jnp.float32) * (1.0 / 16.0)).astype(jnp.bfloat16)
                 for i, b in enumerate(RIGHT_AT[d]):
@@ -292,7 +296,7 @@
         inverse = 1.0 / lev
         for a in range(4):
             block = (carried[a] * inverse).astype(jnp.bfloat16).astype(jnp.float32)
-            new_left[a, :, span] = (block * upright(levels[8 * CHARGE[a]:8 * CHARGE[a] + 1, :])).astype(jnp.bfloat16)
+            new_left[half, a] = (block * upright(levels[8 * CHARGE[a]:8 * CHARGE[a] + 1, :])).astype(jnp.bfloat16)
 
         @pl.when(last)
         def _():
@@ -312,11 +316,10 @@
     invert_leaf(work)
     first = work[...]
     top = dot(first, proj[:h, :], NN)
-    top_iso = right_half(0, top)
+    left_half(0, right_half(0, top))
     lower = dot(gram[h:, :h], first, NT)
     work[...] = gram[h:, h:] - dot(lower, lower, NT)
     proj[h:, :] = proj[h:, :] - dot(lower, top, NN)
-    left_half(0, top_iso)
     invert_leaf(work)
     left_half(1, right_half(1, dot(work[...], proj[h:, :], NN)))
 
@@ -342,7 +345,8 @@
         in_specs=[pl.BlockSpec(memory_space=pltpu.HBM)] * 3 + [pl.BlockSpec(memory_space=pltpu.SMEM)],
         out_specs=(pl.BlockSpec(memory_space=pl.ANY), vmem),
         scratch_shapes=[
-            blocks(10), blocks(10), rows(72), rows(24), rows(8), rows(24), blocks(4), blocks(4), rows(8),
+            blocks(10), pltpu.VMEM((2, 10, n, n // 2), jnp.bfloat16), rows(72), rows(24), rows(8), rows(24),
+            pltpu.VMEM((2, 4, n, n // 2), jnp.bfloat16), blocks(4), rows(8),
             blocks(len(PAIRS)),
             blocks(4),
             pltpu.VMEM((4 * n, 4 * n), jnp.bfloat16),

time: 84.9 us -> 85.2 us (level); the launches traced: 84.7 us -> 83.5 us
  Pallas kernels: 82.1 us -> 80.9 us
    pallas_call x1, Pallas kernels: 82.1 us -> 80.9 us  [per_device(): pl.pallas_call(body, out_shape=(jax.ShapeDtypeStruct(site_blocks.shape, j...]
where the time goes in v4:
time: 85.2 us; the launch traced here: 83.5 us
  Pallas kernels  80.9 us (95%)
  local copies, waits for them, and re-layouts  1.36 us (2%)
  between operations  1.29 us (2%)
    pallas_call x1, Pallas kernels, per_device(): pl.pallas_call(body, out_shape=(jax.ShapeDtypeStruct(site_blocks.shape, j...  80.9 us

profile of v4, /device:TPU:1, one launch (start us, length us, event | category | flops | bytes accessed | tf_op | source)
XLA Modules:
  0.0 83.5 jit_solution(1228813872786099151)
XLA Ops:
  1.3 80.9 %shard_map.59 = (bf16[1,1,4,256,256]{4,3,2,1,0:T(8,128)(2,1)S(1)}, f32[1,1,256]{2,1,0:T(1,128)S(1)}) custom-call(bf16[1,1,4,256,256]{4,3,2,1,0:T(8,128)(2,1)} %site.1, f32[1,1,256]{2,1,0:T(1,128)} %weights_in.1, f32[1,16,16]{2,1,0:T(8,128)} %gates_in.1, s32[1,1]{1,0:T(1,128)S(6)} %copy.8.kept_in), custom_call_target="tpu_custom_call" | custom-call | tf_op jit(solution)/shard_map/pallas_call | solution.py:339
  82.2 0.8 copy.9
  83.0 0.6 copy.10
